TPU v7x, 32 devices: a whole 2x2x4 slice. The times are simulated.
32 devices in a mesh: tm: 16 (over z, y, core), rows: 2 (over x).
Axes of the slice: x: 2, y: 2, z: 4, core: 2. Of those that a mesh axis runs over, the one named last changes fastest.
Arguments:
- noisy_states: float32 [64, 2, 16, 256], P('tm', None, 'rows'), may hold values from -6 to 6
- noise_first: float32 [64, 2, 16, 256], P('tm', None, 'rows'), may hold values from -6 to 6
- noise_second: float32 [64, 2, 16, 256], P('tm', None, 'rows'), may hold values from -6 to 6
- conv_in: bfloat16 [9, 96, 18], replicated, may hold values from -0.5 to 0.5
- conv_out: bfloat16 [9, 2, 96], replicated, may hold values from -0.21875 to 0.21875
- level_embed: float32 [96], replicated, may hold values from -4 to 4
- obs_count: int32 [16, 2], P('tm', 'rows'), may hold values from 1 to 256, as said below
- obs_step: int32 [16, 2, 256], P('tm', 'rows'), may hold values from 0 to 3
- obs_row: int32 [16, 2, 256], P('tm', 'rows'), may hold values from 0 to 7
- obs_col: int32 [16, 2, 256], P('tm', 'rows'), may hold values from 0 to 255
- obs_value: float32 [16, 2, 256], P('tm', 'rows'), may hold values from -4 to 4
Outputs:
- final_states: float32 [64, 2, 16, 256], P('tm', None, 'rows')
Inputs may be any that keep to these rules, and one draw needn't show every extreme that they name: `obs_count`: some block has exactly 256 live observations in every draw; the counts are skewed over blocks.
All inputs are finite; a program needn't handle non-finite values.
Results may differ from a plain program's by a relative error of at most 0.0014.
Values may be sent and summed in bfloat16 or wider, within the bound.
No kernel may reach another device: no remote copies, remote signals or barrier semaphores. Data moves between devices by JAX's collectives and lax.ppermute only.
A program may use at most 64 MiB of HBM per device.

v0:
```python
import functools

import jax
import jax.numpy as jnp
from jax import lax
from jax.experimental import pallas as pl
from jax.experimental.pallas import tpu as pltpu
from jax.sharding import PartitionSpec as P


LEVELS = (1.0, 0.5, 0.2)
OBS_NOISE = 0.1
COVARIANCE_GAIN = 0.5

FL = 8
ROWS = 8
COLS = 256
HID = 96
FRAMES = 4
NEAR = 48
FAR = 32
TAPS = 18
TAP_ROWS = 24
DEPTH = 3 * (NEAR + FAR)
EDGE = 4 * FL
AUX_OBS = 2 * EDGE
AUX_ROWS = AUX_OBS + 16
NO_CELL = 64
AHEAD, LAG2, LAG3 = 4, 4, 4
GROW = (1.0 + LEVELS[0] ** 2) ** 0.5
VMEM = pl.BlockSpec(memory_space=pltpu.VMEM)
F32 = jnp.float32
BF16 = jnp.bfloat16


def params():
    return pltpu.CompilerParams(vmem_limit_bytes=16 * 1024 * 1024)


def iota(shape, dim):
    return lax.broadcasted_iota(jnp.int32, shape, dim)


def split_halves(ref, halves_ref):
    halves_ref[0 : ROWS * FL, :] = ref[:, 0:128].astype(F32)
    halves_ref[ROWS * FL :, :] = ref[:, 128:256].astype(F32)


def row_of(halves_ref, row):
    left = halves_ref[pl.ds(row, FL, stride=ROWS), :]
    right = halves_ref[pl.ds(ROWS * FL + row, FL, stride=ROWS), :]
    return jnp.concatenate([left, right], axis=1)


def pack_kernel(scaled_in, msg_ref, scaled_ref):
    split_halves(scaled_in, scaled_ref)
    for row in range(0, ROWS, 2):
        pair = jnp.concatenate([row_of(scaled_ref, row), row_of(scaled_ref, row + 1)], axis=0)
        msg_ref[row * FL : (row + 2) * FL, :] = pair.astype(BF16)


def aux_kernel(
    count_ref, msg_ref, x_in, noise_in, step_ref, row_ref, col_ref, val_ref, aux_ref, x_ref,
    noise_ref, x_halves, noise_halves,
):
    split_halves(x_in, x_halves)
    split_halves(noise_in, noise_halves)
    for row in range(ROWS):
        x_ref[row * FL : (row + 1) * FL, :] = row_of(x_halves, row)
        noise_ref[row * FL : (row + 1) * FL, :] = row_of(noise_halves, row)
    for at, row in enumerate((0, ROWS - 2)):
        pair = slice(row * FL, (row + 2) * FL)
        rest = x_ref[pair, :] - msg_ref[pair, :].astype(F32) * GROW
        for part, value in enumerate((noise_ref[pair, :], rest)):
            start = part * EDGE + 2 * at * FL
            aux_ref[start : start + 2 * FL, :] = value.astype(BF16)
    live = iota((1, COLS), 1) < count_ref[...]
    cell = jnp.where(live, row_ref[...] * FL + step_ref[...] * 2, NO_CELL).astype(F32)
    val = val_ref[...]
    high = val.astype(BF16).astype(F32)
    middle = (val - high).astype(BF16).astype(F32)
    low = val - high - middle
    which = iota((16, COLS), 0)
    table = jnp.zeros((16, COLS), F32)
    for at, line in enumerate((cell, col_ref[...].astype(F32), high, middle, low)):
        table = jnp.where(which == at, line, table)
    aux_ref[AUX_OBS:AUX_ROWS, :] = table.astype(BF16)


def weights_kernel(n_tm, taps_ref, conv_out_ref, embed_ref, w1_ref, w2_ref, wide_ref):
    here = lax.axis_index("tm")
    even = lax.rem(here, 2) == 0
    has_far = jnp.logical_and(here > 0, here < n_tm - 1)
    wide_ref[...] = jnp.zeros(wide_ref.shape, F32)
    for at in range(9):
        tap = taps_ref[at].astype(F32)
        for frame in range(FRAMES):
            start = at * TAP_ROWS + 2 * frame
            wide_ref[start : start + TAPS, frame * 128 : frame * 128 + HID] = tap
    square = iota((HID, 128), 0) == iota((HID, 128), 1)
    line = jnp.concatenate([embed_ref[...], jnp.zeros((1, 128 - HID), F32)], axis=1)
    embed = jnp.sum(jnp.where(square, line, 0.0), axis=1, keepdims=True)
    high = embed.astype(BF16).astype(F32)
    middle = (embed - high).astype(BF16).astype(F32)
    low = embed - high - middle
    lane = iota((HID, DEPTH), 1) - (3 * NEAR + 3 * FL)
    bias = jnp.where(lane == 0, high, 0.0)
    bias = jnp.where(lane == 1, middle, bias)
    bias = jnp.where(lane == 2, low, bias)
    shape = (TAP_ROWS, DEPTH)
    lanes = iota(shape, 1)
    group = iota(shape, 0) >> 3
    within = iota(shape, 0) & 7
    slot = jnp.where(even, 2 - group, group)
    near = slot * FL + within
    far = jnp.where(has_far, 3 * NEAR + within, -DEPTH)
    parts = []
    for at in range(9):
        row_off, col_off = at // 3, at % 3
        near_start = row_off * NEAR + col_off * 2 * FL
        far_start = row_off * FAR + col_off * FL
        target = jnp.where(slot == 2, far + far_start, near + near_start)
        parts.append(jnp.where(lanes == target, 0.5, 0.0))
    move = jnp.concatenate(parts, axis=0).astype(BF16)
    for frame in range(FRAMES):
        taps = wide_ref[:, frame * 128 : (frame + 1) * 128].T[0:HID, :].astype(BF16)
        out = jnp.dot(taps, move, preferred_element_type=F32)
        w1_ref[frame * HID : (frame + 1) * HID, :] = (out + 0.5 * bias).astype(BF16)
    odd = iota((FL, HID), 0) % 2 == 1
    parts = []
    for at in range(9):
        upper = conv_out_ref[at, 0:1, :].astype(F32)
        lower = conv_out_ref[at, 1:2, :].astype(F32)
        parts.append(jnp.where(odd, lower, upper))
    stacked = jnp.concatenate(parts, axis=0).astype(BF16)
    shape = (HID, FRAMES * HID)
    spread = jnp.where(iota(shape, 1) % HID == iota(shape, 0), 1.0, 0.0).astype(BF16)
    tiled = jnp.dot(stacked, spread, preferred_element_type=F32)
    mine = (iota(tiled.shape, 0) % FL) // 2 == iota(tiled.shape, 1) // HID
    w2_ref[...] = jnp.where(mine, tiled, 0.0).astype(BF16)


def one_hot_maps(table, first_cell, cells):
    shape = (cells, COLS)
    hit = (iota(shape, 0) + first_cell).astype(F32) == table[0:1, :]
    lines = [jnp.where(hit, 1.0, 0.0)]
    for at in (2, 3, 4):
        lines.append(jnp.where(hit, table[at : at + 1, :], 0.0))
    lhs = jnp.concatenate(lines, axis=0).astype(BF16)
    cols_hot = jnp.where(iota((COLS, COLS), 0).astype(F32) == table[1:2, :], 1.0, 0.0)
    out = lax.dot_general(
        lhs, cols_hot.astype(BF16), (((1,), (1,)), ((), ())), preferred_element_type=F32
    )
    count = out[0:cells]
    total = out[cells : 2 * cells] + out[2 * cells : 3 * cells] + out[3 * cells : 4 * cells]
    return count, total


def maps_kernel(msg_ref, up_ref, down_ref, count_ref, total_ref):
    obs = slice(AUX_OBS, AUX_ROWS)
    pieces = (
        (up_ref, (ROWS - 2) * FL, 2 * FL, 0),
        (msg_ref, 0, ROWS * FL, 2 * FL),
        (down_ref, 0, 2 * FL, (ROWS + 2) * FL),
    )
    for ref, first_cell, cells, at in pieces:
        count, total = one_hot_maps(ref[obs, :].astype(F32), first_cell, cells)
        count_ref[at : at + cells, :] = count
        total_ref[at : at + cells, :] = total


def shifts(here):
    return [pltpu.roll(here, 1, 1), here, pltpu.roll(here, COLS - 1, 1)]


def near_kernel(core_ref, own_ref, near_ref):
    for pair in range(own_ref.shape[0] // (2 * FL)):
        at = slice(2 * pair * FL, 2 * (pair + 1) * FL)
        core, own = core_ref[at, :].astype(F32), own_ref[at, :].astype(F32)
        for sub in range(2):
            part = slice(sub * FL, (sub + 1) * FL)
            here = jnp.concatenate([core[part], own[part]], axis=0)
            block = jnp.concatenate(shifts(here), axis=0)
            start = (2 * pair + sub) * NEAR
            near_ref[start : start + NEAR, :] = block.astype(BF16)


def fill_pair(ref, win_ref, pair, level):
    far = ref[2 * pair * FL : 2 * (pair + 1) * FL, :].astype(F32)
    const = jnp.full((FL, COLS), level, F32)
    for sub in range(2):
        here = far[sub * FL : (sub + 1) * FL]
        block = jnp.concatenate(shifts(here) + [const], axis=0)
        start = (2 * pair + sub) * FAR
        win_ref[start : start + FAR, :] = block.astype(BF16)


def run_rows(near_ref, far_ref, w1_ref, w2_ref, win_ref, hid_ref, prod_ref, rows, level, emit):
    hidden_rows = rows - 2
    n = FRAMES * HID
    filled = 0
    for step in range(hidden_rows + LAG2 + LAG3):
        want = min(rows, step + 3 + AHEAD)
        while 2 * filled < want:
            fill_pair(far_ref, win_ref, filled, level)
            filled += 1
        if step < hidden_rows:
            near = near_ref[step * NEAR : (step + 3) * NEAR, :]
            far = win_ref[step * FAR : (step + 3) * FAR, :]
            window = jnp.concatenate([near, far], axis=0)
            half = jnp.dot(w1_ref[...], window, preferred_element_type=F32)
            hid_ref[step * n : (step + 1) * n, :] = (half + half * jnp.tanh(half)).astype(BF16)
        row = step - LAG2
        if 0 <= row < hidden_rows:
            prod_ref[row * 72 : (row + 1) * 72, :] = jnp.dot(
                w2_ref[...], hid_ref[row * n : (row + 1) * n, :], preferred_element_type=F32
            )
        row = step - LAG2 - LAG3
        if row >= 2:
            emit(row - 2)


def net_row(prod_ref, row):
    sums = []
    for col_off in range(3):
        acc = None
        for row_off in range(3):
            at = (row + row_off) * 72 + (3 * row_off + col_off) * FL
            term = prod_ref[at : at + FL, :]
            acc = term if acc is None else acc + term
        sums.append(acc)
    return pltpu.roll(sums[0], 1, 1) + sums[1] + pltpu.roll(sums[2], COLS - 1, 1)


def advance(x, noise, net, count, total, index):
    level, after = LEVELS[index], LEVELS[index + 1]
    spread = level**2 - after**2
    denoised = x * (1.0 / (1.0 + level**2)) + (level / (1.0 + level**2) ** 0.5) * net
    guide = (total - count * denoised) * (1.0 / (OBS_NOISE + COVARIANCE_GAIN * level**2))
    score = (denoised - x) * (1.0 / level**2) + guide
    return x + spread * score + spread**0.5 * noise


def first_kernel(
    x_ref, noise_ref, aux_up_ref, aux_down_ref, near_ref, own_ref, far_ref, w1_ref, w2_ref,
    count_ref, total_ref, next_ref, send_ref, win_ref, hid_ref, prod_ref,
):
    shrink = 1.0 / (1.0 + LEVELS[1] ** 2) ** 0.5
    made = {}

    def emit(here):
        part = slice((here % 2) * FL, (here % 2 + 1) * FL)
        if not 2 <= here < ROWS + 2:
            at = (here + 2) // 2 * 2 * FL
            ref, start = (aux_up_ref, 2 * FL) if here < 2 else (aux_down_ref, 0)
            noise, rest = (
                ref[start + piece * EDGE : start + piece * EDGE + 2 * FL, :].astype(F32)[part]
                for piece in range(2)
            )
            x = own_ref[at : at + 2 * FL, :].astype(F32)[part] * GROW + rest
        else:
            inner = slice((here - 2) * FL, (here - 1) * FL)
            x, noise = x_ref[inner, :], noise_ref[inner, :]
        at = slice(here * FL, (here + 1) * FL)
        new = advance(x, noise, net_row(prod_ref, here), count_ref[at, :], total_ref[at, :], 0)
        if 2 <= here < ROWS + 2:
            next_ref[(here - 2) * FL : (here - 1) * FL, :] = new
        made[here % 2] = new
        if here % 2:
            pair = jnp.concatenate([made[0], made[1]], axis=0) * shrink
            send_ref[(here - 1) * FL : (here + 1) * FL, :] = pair.astype(BF16)

    run_rows(
        near_ref, far_ref, w1_ref, w2_ref, win_ref, hid_ref, prod_ref, 2 * ROWS, LEVELS[0], emit
    )


def second_kernel(
    x_ref, noise_in, near_ref, far_ref, w1_ref, w2_ref,
    count_ref, total_ref, out_ref, win_ref, hid_ref, prod_ref, noise_ref, half_ref,
):
    split_halves(noise_in, noise_ref)

    def emit(row):
        at = slice((row + 2) * FL, (row + 3) * FL)
        new = advance(
            x_ref[row * FL : (row + 1) * FL, :], row_of(noise_ref, row), net_row(prod_ref, row),
            count_ref[at, :], total_ref[at, :], 1,
        )
        half_ref[pl.ds(row, FL, stride=ROWS), :] = new[:, 0:128]
        half_ref[pl.ds(ROWS * FL + row, FL, stride=ROWS), :] = new[:, 128:256]

    run_rows(
        near_ref, far_ref, w1_ref, w2_ref, win_ref, hid_ref, prod_ref, ROWS + 4, LEVELS[1], emit
    )
    out_ref[:, 0:128] = half_ref[0 : ROWS * FL, :]
    out_ref[:, 128:256] = half_ref[ROWS * FL :, :]


def call(kernel, args, specs, outs, scratch=(), flops=0):
    moved = sum(a.size * a.dtype.itemsize for a in args)
    moved += sum(o.size * o.dtype.itemsize for o in outs)
    return pl.pallas_call(
        kernel,
        out_shape=tuple(outs),
        in_specs=specs,
        out_specs=tuple([VMEM] * len(outs)),
        scratch_shapes=list(scratch),
        compiler_params=params(),
        cost_estimate=pl.CostEstimate(flops=flops, bytes_accessed=moved, transcendentals=0),
    )(*args)


def time_pairs(n_tm, n_rows):
    core, far = [], []
    at = lambda i, r: i * n_rows + r
    for r in range(n_rows):
        for i in range(0, n_tm, 2):
            core += [(at(i, r), at(i + 1, r)), (at(i + 1, r), at(i, r))]
        for i in range(1, n_tm - 1, 2):
            far += [(at(i, r), at(i + 1, r)), (at(i + 1, r), at(i, r))]
        for i in (0, n_tm - 1):
            far.append((at(i, r), at(i, r ^ 1)))
    return core, far


def exchange_rows(block, n_rows):
    up = lax.ppermute(block, "rows", [(i, (i + 1) % n_rows) for i in range(n_rows)])
    if n_rows == 2:
        return up, up
    return up, lax.ppermute(block, "rows", [((i + 1) % n_rows, i) for i in range(n_rows)])


def exchange_time(block, n_tm, n_rows):
    core_pairs, far_pairs = time_pairs(n_tm, n_rows)
    far = lax.ppermute(block, ("tm", "rows"), far_pairs)
    core = lax.ppermute(block, ("tm", "rows"), core_pairs)
    return core, far


def scratch_for(rows):
    halves = pltpu.VMEM((2 * ROWS * FL, 128), F32)
    return [
        pltpu.VMEM((rows * FAR, COLS), BF16),
        pltpu.VMEM(((rows - 2) * FRAMES * HID, COLS), BF16),
        pltpu.VMEM(((rows - 2) * 72, COLS), F32),
        halves,
        halves,
    ]


def near_call(core, own):
    rows = own.shape[0] // FL
    (near,) = call(
        near_kernel, (core, own), [VMEM] * 2, [jax.ShapeDtypeStruct((rows * NEAR, COLS), BF16)]
    )
    return near


def first_call(*args):
    shape = jax.ShapeDtypeStruct
    return call(
        first_kernel,
        args,
        [VMEM] * 11,
        [shape((ROWS * FL, COLS), F32), shape(((ROWS + 4) * FL, COLS), BF16)],
        scratch_for(2 * ROWS)[:3],
        flops=14 * 2 * 256 * 384 * (256 + 72),
    )


def second_call(*args):
    (out,) = call(
        second_kernel,
        args,
        [VMEM] * 8,
        [jax.ShapeDtypeStruct((FL * ROWS, COLS), F32)],
        scratch_for(ROWS + 4),
        flops=10 * 2 * 256 * 384 * (256 + 72),
    )
    return out


def per_device(
    noisy_states, noise_first, noise_second, conv_in, conv_out, level_embed,
    obs_count, obs_step, obs_row, obs_col, obs_value,
):
    n_tm, n_rows = lax.axis_size("tm"), lax.axis_size("rows")
    frames, layers, rows, cols = noisy_states.shape
    assert frames == FRAMES and frames * layers == FL and rows == ROWS and cols == COLS
    assert n_tm % 2 == 0 and n_rows % 2 == 0 and obs_step.shape[-1] == COLS
    flat = lambda a: a.reshape(FL * ROWS, COLS)
    line = lambda a: a.reshape(1, -1)
    x, noise_a, noise_b = flat(noisy_states), flat(noise_first), flat(noise_second)
    shape = jax.ShapeDtypeStruct
    scaled = (x / (1.0 + LEVELS[0] ** 2) ** 0.5).astype(BF16)
    halves = pltpu.VMEM((2 * ROWS * FL, 128), F32)
    (msg,) = call(pack_kernel, (scaled,), [VMEM], [shape((ROWS * FL, COLS), BF16)], [halves])
    grid = shape((ROWS * FL, COLS), F32)
    aux, x_rows, noise_rows = call(
        aux_kernel,
        (obs_count, msg, x, noise_a, line(obs_step), line(obs_row), line(obs_col), line(obs_value)),
        [VMEM] * 8,
        [shape((AUX_ROWS, COLS), BF16), grid, grid],
        [halves, halves],
    )
    up, down = exchange_rows(msg, n_rows)
    aux_up, aux_down = exchange_rows(aux, n_rows)
    w1, w2 = call(
        functools.partial(weights_kernel, n_tm),
        (conv_in.transpose(0, 2, 1), conv_out, line(level_embed)),
        [VMEM] * 3,
        [shape((FRAMES * HID, DEPTH), BF16), shape((72, FRAMES * HID), BF16)],
        [pltpu.VMEM((9 * TAP_ROWS, FRAMES * 128), F32)],
    )
    half = ROWS * FL // 2
    own = jnp.concatenate([up[half:], msg, down[:half]], axis=0)
    core, far = exchange_time(own, n_tm, n_rows)
    maps = shape(((ROWS + 4) * FL, COLS), F32)
    count, total = call(maps_kernel, (aux, aux_up, aux_down), [VMEM] * 3, [maps, maps])
    near = near_call(core, own)
    current, send = first_call(
        x_rows, noise_rows, aux_up, aux_down, near, own, far, w1, w2, count, total
    )
    core, far = exchange_time(send, n_tm, n_rows)
    near = near_call(core, send)
    out = second_call(current, noise_b, near, far, w1, w2, count, total)
    return out.reshape(noisy_states.shape)


def solution(mesh):
    states = P("tm", None, "rows", None)
    slots = P("tm", "rows", None)
    in_specs = (states, states, states, P(), P(), P(), P("tm", "rows"), slots, slots, slots, slots)
    return jax.shard_map(
        per_device, mesh=mesh, in_specs=in_specs, out_specs=states, check_vma=False
    )
```

profile of v0, /device:TPU:0, one launch (start us, length us, event | category | flops | bytes accessed | tf_op | source)
XLA Modules:
  0.0 21.5 jit_solution(2272223773559556653)
XLA Ops:
  0.0 0.8 %multiply_convert_fusion.scaled_in = bf16[64,256]{1,0:T(8,128)(2,1)S(1)} fusion(f32[4,2,8,256]{3,2,1,0:T(8,128)} %param.11), kind=kLoop, calls=%fused_computation.1 | loop fusion | flops 32768 | bytes 98304 | tf_op jit(solution)/shard_map/convert_element_type | solution.py:396
  0.9 3.0 %collective-permute-start.1 = (bf16[64,256]{1,0:T(8,128)(2,1)S(1)}, bf16[64,256]{1,0:T(8,128)(2,1)S(1)}, u32[]{:S(2)}, u32[]{:S(2)}) collective-permute-start(bf16[64,256]{1,0:T(8,128)(2,1)S(1)} %shard_map.109.msg_ref), channel_id=1, source_target_pairs={{0,1},{1,0},{2,3},{3,2},{4,5},{5,4},{6,7},{7,6},{8,9},{9,8},{10,11... | collective-permute-start | bytes 98312 | tf_op jit(solution)/shard_map/ppermute | solution.py:328
  3.9 1.9 %collective-permute-done.1 = bf16[64,256]{1,0:T(8,128)(2,1)S(1)} collective-permute-done((bf16[64,256]{1,0:T(8,128)(2,1)S(1)}, bf16[64,256]{1,0:T(8,128)(2,1)S(1)}, u32[]{:S(2)}, u32[]{:S(2)}) %collective-permute-start.1) | collective-permute-done | bytes 32800 | tf_op jit(solution)/shard_map/ppermute | solution.py:328
  5.8 0.0 copy-start
  5.8 0.0 copy-start.1
  5.8 0.1 collective-permute-start.2
  5.9 2.1 %collective-permute-start.3 = (bf16[128,256]{1,0:T(8,128)(2,1)S(1)}, bf16[128,256]{1,0:T(8,128)(2,1)S(1)}, u32[]{:S(2)}, u32[]{:S(2)}) collective-permute-start(bf16[128,256]{1,0:T(8,128)(2,1)S(1)} %pad_maximum_fusion.own_ref), channel_id=1, source_target_pairs={{2,4},{4,2},{6,8},{8,6},{10,12},{12,10},{14,16},{16,14},{18,20},{2... | collective-permute-start | bytes 196616 | tf_op jit(solution)/shard_map/ppermute | solution.py:336
  8.6 0.0 copy-start.5
  8.7 0.0 copy-start.6
  8.7 0.0 copy-start.7
  8.7 0.0 copy-start.4
  8.7 0.0 copy-done
  8.7 0.0 copy-done.1
  8.7 0.6 %copy-done.5 = s32[1,1,256]{2,1,0:T(1,128)S(1)} copy-done((s32[1,1,256]{2,1,0:T(1,128)S(1)}, s32[1,1,256]{2,1,0:T(1,128)}, u32[]{:S(2)}) %copy-start.5) | copy-done | bytes 1048
  9.3 0.0 copy-done.6
  9.3 0.0 copy-done.7
  9.4 0.0 copy-done.4
  9.4 0.0 copy-start.2
  9.4 0.1 shard_map.110
  9.5 0.0 copy-start.3
  9.5 0.1 collective-permute-start
  9.5 0.0 copy-start.8
  9.5 0.6 %copy-done.2 = bf16[9,96,18]{1,2,0:T(8,128)(2,1)S(1)} copy-done((bf16[9,96,18]{1,2,0:T(8,128)(2,1)S(1)}, bf16[9,96,18]{1,2,0:T(8,128)(2,1)}, u32[]{:S(2)}) %copy-start.2) | copy-done | bytes 31128
  10.2 0.0 copy-done.3
  10.2 0.0 copy-done.8
  10.2 0.3 %shard_map.112 = (bf16[384,240]{1,0:T(8,128)(2,1)S(1)}, bf16[72,384]{1,0:T(8,128)(2,1)S(1)}) custom-call(bf16[9,18,96]{2,1,0:T(8,128)(2,1)S(1)} %bitcast.13, bf16[9,2,96]{2,1,0:T(2,128)(2,1)S(1)} %copy-done.3, f32[1,96]{1,0:T(1,128)S(1)} %bitcast.18), custom_call_target="tpu_custom_call" | custom-call | bytes 274560 | tf_op jit(solution)/shard_map/pallas_call | solution.py:303
  10.5 3.0 %collective-permute-done.up_ref.down_ref.aux_up_ref.aux_down_ref = bf16[80,256]{1,0:T(8,128)(2,1)S(1)} collective-permute-done((bf16[80,256]{1,0:T(8,128)(2,1)S(1)}, bf16[80,256]{1,0:T(8,128)(2,1)S(1)}, u32[]{:S(2)}, u32[]{:S(2)}) %collective-permute-start) | collective-permute-done | bytes 40992 | tf_op jit(solution)/shard_map/ppermute | solution.py:328
  13.5 0.3 %shard_map.113 = (f32[96,256]{1,0:T(8,128)S(1)}, f32[96,256]{1,0:T(8,128)S(1)}) custom-call(bf16[80,256]{1,0:T(8,128)(2,1)S(1)} %get-tuple-element.16.msg_ref, bf16[80,256]{1,0:T(8,128)(2,1)S(1)} %collective-permute-done.up_ref.down_ref.aux_up_ref.aux_down_ref, bf16[80,256]{1,0:T(8,128)(2,1)S(1)} %collective-permute-done.up_ref.down_ref.aux_up_ref.aux_down_ref), custom_call_target="tpu_custom_call" | custom-call | bytes 319488 | tf_op jit(solution)/shard_map/pallas_call | solution.py:303
  13.8 0.0 collective-permute-done.2.core_ref
  13.8 0.1 shard_map.111.near_ref
  13.9 0.0 collective-permute-done.3.far_ref
  14.0 1.5 %shard_map.114 = (f32[64,256]{1,0:T(8,128)S(1)}, bf16[96,256]{1,0:T(8,128)(2,1)S(1)}) custom-call(f32[64,256]{1,0:T(8,128)S(1)} %get-tuple-element.14.x_ref, f32[64,256]{1,0:T(8,128)S(1)} %get-tuple-element.15.noise_ref, bf16[80,256]{1,0:T(8,128)(2,1)S(1)} %collective-permute-done.up_ref.down_ref.aux_up_ref.aux_down_ref, ...), custom_call_target="tpu_custom_call" | custom-call | flops 902823936 | bytes 1288192 | tf_op jit(solution)/shard_map/pallas_call | solution.py:303
  15.5 0.0 copy-start.9
  15.5 0.1 collective-permute-start.4
  15.6 0.5 %collective-permute-start.5 = (bf16[96,256]{1,0:T(8,128)(2,1)S(1)}, bf16[96,256]{1,0:T(8,128)(2,1)S(1)}, u32[]{:S(2)}, u32[]{:S(2)}) collective-permute-start(bf16[96,256]{1,0:T(8,128)(2,1)S(1)} %get-tuple-element.22.own_ref), channel_id=1, source_target_pairs={{2,4},{4,2},{6,8},{8,6},{10,12},{12,10},{14,16},{16,14},{18,20},{2... | collective-permute-start | bytes 147464 | tf_op jit(solution)/shard_map/ppermute | solution.py:336
  16.0 0.7 %collective-permute-done.4.core_ref = bf16[96,256]{1,0:T(8,128)(2,1)S(1)} collective-permute-done((bf16[96,256]{1,0:T(8,128)(2,1)S(1)}, bf16[96,256]{1,0:T(8,128)(2,1)S(1)}, u32[]{:S(2)}, u32[]{:S(2)}) %collective-permute-start.4) | collective-permute-done | bytes 49184 | tf_op jit(solution)/shard_map/ppermute | solution.py:337
  16.8 0.1 shard_map.115.near_ref
  16.9 2.8 %collective-permute-done.5.far_ref = bf16[96,256]{1,0:T(8,128)(2,1)S(1)} collective-permute-done((bf16[96,256]{1,0:T(8,128)(2,1)S(1)}, bf16[96,256]{1,0:T(8,128)(2,1)S(1)}, u32[]{:S(2)}, u32[]{:S(2)}) %collective-permute-start.5) | collective-permute-done | bytes 49184 | tf_op jit(solution)/shard_map/ppermute | solution.py:336
  19.7 0.0 copy-done.9
  19.7 1.8 %shard_map.116 = f32[64,256]{1,0:T(8,128)} custom-call(f32[64,256]{1,0:T(8,128)S(1)} %get-tuple-element.21.x_ref, f32[64,256]{1,0:T(8,128)S(1)} %bitcast.19, bf16[576,256]{1,0:T(8,128)(2,1)S(1)} %shard_map.115.near_ref, bf16[96,256]{1,0:T(8,128)(2,1)S(1)} %collective-permute-done.5.far_ref, bf16[384,240]{1,0:T(8,128)(2,1)S(1)} %get-tuple-element.17.w1_ref, ...), custom_call_target="tpu_custom_call" | custom-call | flops 644874240 | bytes 976896 | tf_op jit(solution)/shard_map/pallas_call | solution.py:303
  (3 shorter events, 0.0 us)
Async XLA Ops:
  0.9 4.9 %collective-permute-start.1 = (bf16[64,256]{1,0:T(8,128)(2,1)S(1)}, bf16[64,256]{1,0:T(8,128)(2,1)S(1)}, u32[]{:S(2)}, u32[]{:S(2)}) collective-permute-start(bf16[64,256]{1,0:T(8,128)(2,1)S(1)} %shard_map.109.msg_ref), channel_id=1, source_target_pairs={{0,1},{1,0},{2,3},{3,2},{4,5},{5,4},{6,7},{7,6},{8,9},{9,8},{10,11... | collective-permute-start | bytes 98312 | tf_op jit(solution)/shard_map/ppermute | solution.py:328
  5.8 2.9 %copy-start = (f32[4,2,8,256]{3,2,1,0:T(8,128)S(1)}, f32[4,2,8,256]{3,2,1,0:T(8,128)}, u32[]{:S(2)}) copy-start(f32[4,2,8,256]{3,2,1,0:T(8,128)} %param.11) | copy-start | bytes 196612
  5.8 2.9 %copy-start.1 = (f32[4,2,8,256]{3,2,1,0:T(8,128)S(1)}, f32[4,2,8,256]{3,2,1,0:T(8,128)}, u32[]{:S(2)}) copy-start(f32[4,2,8,256]{3,2,1,0:T(8,128)} %param.12) | copy-start | bytes 196612
  5.8 8.0 %collective-permute-start.2 = (bf16[128,256]{1,0:T(8,128)(2,1)S(1)}, bf16[128,256]{1,0:T(8,128)(2,1)S(1)}, u32[]{:S(2)}, u32[]{:S(2)}) collective-permute-start(bf16[128,256]{1,0:T(8,128)(2,1)S(1)} %pad_maximum_fusion.own_ref), channel_id=1, source_target_pairs={{0,2},{2,0},{4,6},{6,4},{8,10},{10,8},{12,14},{14,12},{16,18},{18,... | collective-permute-start | bytes 196616 | tf_op jit(solution)/shard_map/ppermute | solution.py:337
  5.9 8.0 %collective-permute-start.3 = (bf16[128,256]{1,0:T(8,128)(2,1)S(1)}, bf16[128,256]{1,0:T(8,128)(2,1)S(1)}, u32[]{:S(2)}, u32[]{:S(2)}) collective-permute-start(bf16[128,256]{1,0:T(8,128)(2,1)S(1)} %pad_maximum_fusion.own_ref), channel_id=1, source_target_pairs={{2,4},{4,2},{6,8},{8,6},{10,12},{12,10},{14,16},{16,14},{18,20},{2... | collective-permute-start | bytes 196616 | tf_op jit(solution)/shard_map/ppermute | solution.py:336
  8.6 0.7 %copy-start.5 = (s32[1,1,256]{2,1,0:T(1,128)S(1)}, s32[1,1,256]{2,1,0:T(1,128)}, u32[]{:S(2)}) copy-start(s32[1,1,256]{2,1,0:T(1,128)} %param.19) | copy-start | bytes 3076
  8.7 0.7 %copy-start.6 = (s32[1,1,256]{2,1,0:T(1,128)S(1)}, s32[1,1,256]{2,1,0:T(1,128)}, u32[]{:S(2)}) copy-start(s32[1,1,256]{2,1,0:T(1,128)} %param.20) | copy-start | bytes 3076
  8.7 0.7 %copy-start.7 = (f32[1,1,256]{2,1,0:T(1,128)S(1)}, f32[1,1,256]{2,1,0:T(1,128)}, u32[]{:S(2)}) copy-start(f32[1,1,256]{2,1,0:T(1,128)} %param.21) | copy-start | bytes 3076
  8.7 0.7 %copy-start.4 = (s32[1,1,256]{2,1,0:T(1,128)S(1)}, s32[1,1,256]{2,1,0:T(1,128)}, u32[]{:S(2)}) copy-start(s32[1,1,256]{2,1,0:T(1,128)} %param.18) | copy-start | bytes 3076
  9.4 0.8 %copy-start.2 = (bf16[9,96,18]{1,2,0:T(8,128)(2,1)S(1)}, bf16[9,96,18]{1,2,0:T(8,128)(2,1)}, u32[]{:S(2)}) copy-start(bf16[9,96,18]{1,2,0:T(8,128)(2,1)} %param.14) | copy-start | bytes 93316
  9.5 0.7 %copy-start.3 = (bf16[9,2,96]{2,1,0:T(2,128)(2,1)S(1)}, bf16[9,2,96]{2,1,0:T(2,128)(2,1)}, u32[]{:S(2)}) copy-start(bf16[9,2,96]{2,1,0:T(2,128)(2,1)} %conv_out_ref.1) | copy-start | bytes 10372
  9.5 4.1 %collective-permute-start = (bf16[80,256]{1,0:T(8,128)(2,1)S(1)}, bf16[80,256]{1,0:T(8,128)(2,1)S(1)}, u32[]{:S(2)}, u32[]{:S(2)}) collective-permute-start(bf16[80,256]{1,0:T(8,128)(2,1)S(1)} %get-tuple-element.16.msg_ref), channel_id=1, source_target_pairs={{0,1},{1,0},{2,3},{3,2},{4,5},{5,4},{6,7},{7,6},{8,9},{9,8},{10,11... | collective-permute-start | bytes 122888 | tf_op jit(solution)/shard_map/ppermute | solution.py:328
  9.5 0.7 %copy-start.8 = (f32[96]{0:T(128)S(1)}, f32[96]{0:T(128)}, u32[]{:S(2)}) copy-start(f32[96]{0:T(128)} %param.16) | copy-start | bytes 1156
  15.5 4.2 %copy-start.9 = (f32[4,2,8,256]{3,2,1,0:T(8,128)S(1)}, f32[4,2,8,256]{3,2,1,0:T(8,128)}, u32[]{:S(2)}) copy-start(f32[4,2,8,256]{3,2,1,0:T(8,128)} %param.13) | copy-start | bytes 196612
  15.5 1.3 %collective-permute-start.4 = (bf16[96,256]{1,0:T(8,128)(2,1)S(1)}, bf16[96,256]{1,0:T(8,128)(2,1)S(1)}, u32[]{:S(2)}, u32[]{:S(2)}) collective-permute-start(bf16[96,256]{1,0:T(8,128)(2,1)S(1)} %get-tuple-element.22.own_ref), channel_id=1, source_target_pairs={{0,2},{2,0},{4,6},{6,4},{8,10},{10,8},{12,14},{14,12},{16,18},{18,... | collective-permute-start | bytes 147464 | tf_op jit(solution)/shard_map/ppermute | solution.py:337
  15.6 4.2 %collective-permute-start.5 = (bf16[96,256]{1,0:T(8,128)(2,1)S(1)}, bf16[96,256]{1,0:T(8,128)(2,1)S(1)}, u32[]{:S(2)}, u32[]{:S(2)}) collective-permute-start(bf16[96,256]{1,0:T(8,128)(2,1)S(1)} %get-tuple-element.22.own_ref), channel_id=1, source_target_pairs={{2,4},{4,2},{6,8},{8,6},{10,12},{12,10},{14,16},{16,14},{18,20},{2... | collective-permute-start | bytes 147464 | tf_op jit(solution)/shard_map/ppermute | solution.py:336
where the time goes:
time: 21.7 us; the launch traced here: 21.5 us
  waiting for transfers between devices  8.43 us (39%)
  starting transfers between devices  5.79 us (27%)
  Pallas kernels  4.28 us (20%)
  local copies, waits for them, and re-layouts  1.35 us (6%)
  other arithmetic  0.85 us (4%)
  between operations  0.8 us (4%)
    ppermute x2, waiting for transfers between devices, exchange_rows(): lax.ppermute(block, 'rows', [(i, (i + 1) % n_rows) for i in range(n_rows)])  4.87 us
    pallas_call x8, Pallas kernels, call(): pl.pallas_call(kernel, out_shape=tuple(outs), in_specs=specs, out_specs=t...  4.28 us
    ppermute x2, starting transfers between devices, exchange_rows(): lax.ppermute(block, 'rows', [(i, (i + 1) % n_rows) for i in range(n_rows)])  3.1 us
    ppermute x2, waiting for transfers between devices, exchange_time(): far = lax.ppermute(block, ('tm', 'rows'), far_pairs)  2.81 us
    ppermute x2, starting transfers between devices, exchange_time(): far = lax.ppermute(block, ('tm', 'rows'), far_pairs)  2.56 us
    unnamed x20, local copies, waits for them, and re-layouts  1.35 us
    convert_element_type x1, other arithmetic, per_device(): scaled = (x / (1.0 + LEVELS[0] ** 2) ** 0.5).astype(BF16)  0.85 us
    ppermute x2, waiting for transfers between devices, exchange_time(): core = lax.ppermute(block, ('tm', 'rows'), core_pairs)  0.75 us
  transfers between devices with their start and end apart: 6, of which 4 were waited for; matrix products, arithmetic and copies ran while one was open for 0% of the time, Pallas kernels for 4%

commit v1 on v0

--- a/solution.py
+++ b/solution.py
@@ -22,12 +22,10 @@
 TAPS = 18
 TAP_ROWS = 24
 DEPTH = 3 * (NEAR + FAR)
-EDGE = 4 * FL
-AUX_OBS = 2 * EDGE
+AUX_OBS = 4 * FL
 AUX_ROWS = AUX_OBS + 16
 NO_CELL = 64
 AHEAD, LAG2, LAG3 = 4, 4, 4
-GROW = (1.0 + LEVELS[0] ** 2) ** 0.5
 VMEM = pl.BlockSpec(memory_space=pltpu.VMEM)
 F32 = jnp.float32
 BF16 = jnp.bfloat16
@@ -56,12 +54,13 @@
     split_halves(scaled_in, scaled_ref)
     for row in range(0, ROWS, 2):
         pair = jnp.concatenate([row_of(scaled_ref, row), row_of(scaled_ref, row + 1)], axis=0)
+        pair = pair * (1.0 / (1.0 + LEVELS[0] ** 2) ** 0.5)
         msg_ref[row * FL : (row + 2) * FL, :] = pair.astype(BF16)
 
 
 def aux_kernel(
-    count_ref, msg_ref, x_in, noise_in, step_ref, row_ref, col_ref, val_ref, aux_ref, x_ref,
-    noise_ref, x_halves, noise_halves,
+    count_ref, x_in, noise_in, step_ref, row_ref, col_ref, val_ref, aux_ref, x_ref, noise_ref,
+    x_halves, noise_halves,
 ):
     split_halves(x_in, x_halves)
     split_halves(noise_in, noise_halves)
@@ -69,11 +68,8 @@
         x_ref[row * FL : (row + 1) * FL, :] = row_of(x_halves, row)
         noise_ref[row * FL : (row + 1) * FL, :] = row_of(noise_halves, row)
     for at, row in enumerate((0, ROWS - 2)):
-        pair = slice(row * FL, (row + 2) * FL)
-        rest = x_ref[pair, :] - msg_ref[pair, :].astype(F32) * GROW
-        for part, value in enumerate((noise_ref[pair, :], rest)):
-            start = part * EDGE + 2 * at * FL
-            aux_ref[start : start + 2 * FL, :] = value.astype(BF16)
+        pair = noise_ref[row * FL : (row + 2) * FL, :]
+        aux_ref[2 * at * FL : 2 * (at + 1) * FL, :] = pair.astype(BF16)
     live = iota((1, COLS), 1) < count_ref[...]
     cell = jnp.where(live, row_ref[...] * FL + step_ref[...] * 2, NO_CELL).astype(F32)
     val = val_ref[...]
@@ -245,6 +241,7 @@
     x_ref, noise_ref, aux_up_ref, aux_down_ref, near_ref, own_ref, far_ref, w1_ref, w2_ref,
     count_ref, total_ref, next_ref, send_ref, win_ref, hid_ref, prod_ref,
 ):
+    grow = (1.0 + LEVELS[0] ** 2) ** 0.5
     shrink = 1.0 / (1.0 + LEVELS[1] ** 2) ** 0.5
     made = {}
 
@@ -252,12 +249,9 @@
         part = slice((here % 2) * FL, (here % 2 + 1) * FL)
         if not 2 <= here < ROWS + 2:
             at = (here + 2) // 2 * 2 * FL
+            x = own_ref[at : at + 2 * FL, :].astype(F32)[part] * grow
             ref, start = (aux_up_ref, 2 * FL) if here < 2 else (aux_down_ref, 0)
-            noise, rest = (
-                ref[start + piece * EDGE : start + piece * EDGE + 2 * FL, :].astype(F32)[part]
-                for piece in range(2)
-            )
-            x = own_ref[at : at + 2 * FL, :].astype(F32)[part] * GROW + rest
+            noise = ref[start : start + 2 * FL, :].astype(F32)[part]
         else:
             inner = slice((here - 2) * FL, (here - 1) * FL)
             x, noise = x_ref[inner, :], noise_ref[inner, :]
@@ -393,14 +387,13 @@
     line = lambda a: a.reshape(1, -1)
     x, noise_a, noise_b = flat(noisy_states), flat(noise_first), flat(noise_second)
     shape = jax.ShapeDtypeStruct
-    scaled = (x / (1.0 + LEVELS[0] ** 2) ** 0.5).astype(BF16)
     halves = pltpu.VMEM((2 * ROWS * FL, 128), F32)
-    (msg,) = call(pack_kernel, (scaled,), [VMEM], [shape((ROWS * FL, COLS), BF16)], [halves])
+    (msg,) = call(pack_kernel, (x,), [VMEM], [shape((ROWS * FL, COLS), BF16)], [halves])
     grid = shape((ROWS * FL, COLS), F32)
     aux, x_rows, noise_rows = call(
         aux_kernel,
-        (obs_count, msg, x, noise_a, line(obs_step), line(obs_row), line(obs_col), line(obs_value)),
-        [VMEM] * 8,
+        (obs_count, x, noise_a, line(obs_step), line(obs_row), line(obs_col), line(obs_value)),
+        [VMEM] * 7,
         [shape((AUX_ROWS, COLS), BF16), grid, grid],
         [halves, halves],
     )

time: 21.7 us -> 21.6 us (level)
  local copies, waits for them, and re-layouts: 1.35 us -> 2.2 us
  other arithmetic: 0.85 us -> 0.01 us
    unnamed x20, local copies, waits for them, and re-layouts: 1.35 us -> 2.19 us
    convert_element_type x1 -> x0, other arithmetic: 0.85 us -> none  [per_device(): scaled = (x / (1.0 + LEVELS[0] ** 2) ** 0.5).astype(BF16)]
where the time goes in v1:
time: 21.6 us; the launch traced here: 21.3 us
  waiting for transfers between devices  8.26 us (38%)
  starting transfers between devices  5.79 us (27%)
  Pallas kernels  4.29 us (20%)
  local copies, waits for them, and re-layouts  2.2 us (10%)
  between operations  0.79 us (4%)
    ppermute x2, waiting for transfers between devices, exchange_rows(): lax.ppermute(block, 'rows', [(i, (i + 1) % n_rows) for i in range(n_rows)])  4.7 us
    pallas_call x8, Pallas kernels, call(): pl.pallas_call(kernel, out_shape=tuple(outs), in_specs=specs, out_specs=t...  4.29 us
    ppermute x2, starting transfers between devices, exchange_rows(): lax.ppermute(block, 'rows', [(i, (i + 1) % n_rows) for i in range(n_rows)])  3.09 us
    ppermute x2, waiting for transfers between devices, exchange_time(): far = lax.ppermute(block, ('tm', 'rows'), far_pairs)  2.81 us
    ppermute x2, starting transfers between devices, exchange_time(): far = lax.ppermute(block, ('tm', 'rows'), far_pairs)  2.55 us
    unnamed x20, local copies, waits for them, and re-layouts  2.19 us
    ppermute x2, waiting for transfers between devices, exchange_time(): core = lax.ppermute(block, ('tm', 'rows'), core_pairs)  0.75 us
  transfers between devices with their start and end apart: 6, of which 4 were waited for; matrix products, arithmetic and copies ran while one was open for 0% of the time, Pallas kernels for 4%

profile of v1, /device:TPU:0, one launch (start us, length us, event | category | flops | bytes accessed | tf_op | source)
XLA Modules:
  0.0 21.3 jit_solution(12491868400350735103)
XLA Ops:
  0.0 0.0 copy-start
  0.0 0.8 %copy-done = f32[4,2,8,256]{3,2,1,0:T(8,128)S(1)} copy-done((f32[4,2,8,256]{3,2,1,0:T(8,128)S(1)}, f32[4,2,8,256]{3,2,1,0:T(8,128)}, u32[]{:S(2)}) %copy-start) | copy-done | bytes 65560
  0.9 3.0 %collective-permute-start.1 = (bf16[64,256]{1,0:T(8,128)(2,1)S(1)}, bf16[64,256]{1,0:T(8,128)(2,1)S(1)}, u32[]{:S(2)}, u32[]{:S(2)}) collective-permute-start(bf16[64,256]{1,0:T(8,128)(2,1)S(1)} %shard_map.110), channel_id=1, source_target_pairs={{0,1},{1,0},{2,3},{3,2},{4,5},{5,4},{6,7},{7,6},{8,9},{9,8},{10,11... | collective-permute-start | bytes 98312 | tf_op jit(solution)/shard_map/ppermute | solution.py:322
  3.9 1.9 %collective-permute-done.1 = bf16[64,256]{1,0:T(8,128)(2,1)S(1)} collective-permute-done((bf16[64,256]{1,0:T(8,128)(2,1)S(1)}, bf16[64,256]{1,0:T(8,128)(2,1)S(1)}, u32[]{:S(2)}, u32[]{:S(2)}) %collective-permute-start.1) | collective-permute-done | bytes 32800 | tf_op jit(solution)/shard_map/ppermute | solution.py:322
  5.8 0.0 copy-start.1
  5.8 0.1 collective-permute-start.2
  5.9 2.1 %collective-permute-start.3 = (bf16[128,256]{1,0:T(8,128)(2,1)S(1)}, bf16[128,256]{1,0:T(8,128)(2,1)S(1)}, u32[]{:S(2)}, u32[]{:S(2)}) collective-permute-start(bf16[128,256]{1,0:T(8,128)(2,1)S(1)} %pad_maximum_fusion.own_ref), channel_id=1, source_target_pairs={{2,4},{4,2},{6,8},{8,6},{10,12},{12,10},{14,16},{16,14},{18,20},{2... | collective-permute-start | bytes 196616 | tf_op jit(solution)/shard_map/ppermute | solution.py:330
  8.6 0.0 copy-start.5
  8.6 0.0 copy-start.6
  8.6 0.0 copy-start.7
  8.7 0.0 copy-start.4
  8.7 0.0 copy-done.1
  8.7 0.6 %copy-done.5 = s32[1,1,256]{2,1,0:T(1,128)S(1)} copy-done((s32[1,1,256]{2,1,0:T(1,128)S(1)}, s32[1,1,256]{2,1,0:T(1,128)}, u32[]{:S(2)}) %copy-start.5) | copy-done | bytes 1048
  9.3 0.0 copy-done.6
  9.3 0.0 copy-done.7
  9.3 0.0 copy-done.4
  9.4 0.0 copy-start.2
  9.4 0.1 shard_map.109
  9.4 0.0 copy-start.3
  9.4 0.1 collective-permute-start
  9.5 0.0 copy-start.8
  9.5 0.6 %copy-done.2 = bf16[9,96,18]{1,2,0:T(8,128)(2,1)S(1)} copy-done((bf16[9,96,18]{1,2,0:T(8,128)(2,1)S(1)}, bf16[9,96,18]{1,2,0:T(8,128)(2,1)}, u32[]{:S(2)}) %copy-start.2) | copy-done | bytes 31128
  10.2 0.0 copy-done.3
  10.2 0.0 copy-done.8
  10.2 0.3 %shard_map.112 = (bf16[384,240]{1,0:T(8,128)(2,1)S(1)}, bf16[72,384]{1,0:T(8,128)(2,1)S(1)}) custom-call(bf16[9,18,96]{2,1,0:T(8,128)(2,1)S(1)} %bitcast.13, bf16[9,2,96]{2,1,0:T(2,128)(2,1)S(1)} %copy-done.3, f32[1,96]{1,0:T(1,128)S(1)} %bitcast.18), custom_call_target="tpu_custom_call" | custom-call | bytes 274560 | tf_op jit(solution)/shard_map/pallas_call | solution.py:297
  10.5 2.8 %collective-permute-done.up_ref.down_ref.aux_up_ref.aux_down_ref = bf16[48,256]{1,0:T(8,128)(2,1)S(1)} collective-permute-done((bf16[48,256]{1,0:T(8,128)(2,1)S(1)}, bf16[48,256]{1,0:T(8,128)(2,1)S(1)}, u32[]{:S(2)}, u32[]{:S(2)}) %collective-permute-start) | collective-permute-done | bytes 24608 | tf_op jit(solution)/shard_map/ppermute | solution.py:322
  13.3 0.3 %shard_map.113 = (f32[96,256]{1,0:T(8,128)S(1)}, f32[96,256]{1,0:T(8,128)S(1)}) custom-call(bf16[48,256]{1,0:T(8,128)(2,1)S(1)} %get-tuple-element.16.msg_ref, bf16[48,256]{1,0:T(8,128)(2,1)S(1)} %collective-permute-done.up_ref.down_ref.aux_up_ref.aux_down_ref, bf16[48,256]{1,0:T(8,128)(2,1)S(1)} %collective-permute-done.up_ref.down_ref.aux_up_ref.aux_down_ref), custom_call_target="tpu_custom_call" | custom-call | bytes 270336 | tf_op jit(solution)/shard_map/pallas_call | solution.py:297
  13.6 0.0 collective-permute-done.2.core_ref
  13.6 0.1 shard_map.111.near_ref
  13.8 0.0 collective-permute-done.3.far_ref
  13.8 1.5 %shard_map.114 = (f32[64,256]{1,0:T(8,128)S(1)}, bf16[96,256]{1,0:T(8,128)(2,1)S(1)}) custom-call(f32[64,256]{1,0:T(8,128)S(1)} %get-tuple-element.14.x_ref, f32[64,256]{1,0:T(8,128)S(1)} %get-tuple-element.15.noise_ref, bf16[48,256]{1,0:T(8,128)(2,1)S(1)} %collective-permute-done.up_ref.down_ref.aux_up_ref.aux_down_ref, ...), custom_call_target="tpu_custom_call" | custom-call | flops 902823936 | bytes 1255424 | tf_op jit(solution)/shard_map/pallas_call | solution.py:297
  15.3 0.0 copy-start.9
  15.3 0.1 collective-permute-start.4
  15.4 0.5 %collective-permute-start.5 = (bf16[96,256]{1,0:T(8,128)(2,1)S(1)}, bf16[96,256]{1,0:T(8,128)(2,1)S(1)}, u32[]{:S(2)}, u32[]{:S(2)}) collective-permute-start(bf16[96,256]{1,0:T(8,128)(2,1)S(1)} %get-tuple-element.22.own_ref), channel_id=1, source_target_pairs={{2,4},{4,2},{6,8},{8,6},{10,12},{12,10},{14,16},{16,14},{18,20},{2... | collective-permute-start | bytes 147464 | tf_op jit(solution)/shard_map/ppermute | solution.py:330
  15.8 0.7 %collective-permute-done.4.core_ref = bf16[96,256]{1,0:T(8,128)(2,1)S(1)} collective-permute-done((bf16[96,256]{1,0:T(8,128)(2,1)S(1)}, bf16[96,256]{1,0:T(8,128)(2,1)S(1)}, u32[]{:S(2)}, u32[]{:S(2)}) %collective-permute-start.4) | collective-permute-done | bytes 49184 | tf_op jit(solution)/shard_map/ppermute | solution.py:331
  16.6 0.1 shard_map.115.near_ref
  16.7 2.8 %collective-permute-done.5.far_ref = bf16[96,256]{1,0:T(8,128)(2,1)S(1)} collective-permute-done((bf16[96,256]{1,0:T(8,128)(2,1)S(1)}, bf16[96,256]{1,0:T(8,128)(2,1)S(1)}, u32[]{:S(2)}, u32[]{:S(2)}) %collective-permute-start.5) | collective-permute-done | bytes 49184 | tf_op jit(solution)/shard_map/ppermute | solution.py:330
  19.5 0.0 copy-done.9
  19.5 1.8 %shard_map.116 = f32[64,256]{1,0:T(8,128)} custom-call(f32[64,256]{1,0:T(8,128)S(1)} %get-tuple-element.21.x_ref, f32[64,256]{1,0:T(8,128)S(1)} %bitcast.19, bf16[576,256]{1,0:T(8,128)(2,1)S(1)} %shard_map.115.near_ref, bf16[96,256]{1,0:T(8,128)(2,1)S(1)} %collective-permute-done.5.far_ref, bf16[384,240]{1,0:T(8,128)(2,1)S(1)} %get-tuple-element.17.w1_ref, ...), custom_call_target="tpu_custom_call" | custom-call | flops 644874240 | bytes 976896 | tf_op jit(solution)/shard_map/pallas_call | solution.py:297
  (3 shorter events, 0.0 us)
Async XLA Ops:
  0.0 0.8 %copy-start = (f32[4,2,8,256]{3,2,1,0:T(8,128)S(1)}, f32[4,2,8,256]{3,2,1,0:T(8,128)}, u32[]{:S(2)}) copy-start(f32[4,2,8,256]{3,2,1,0:T(8,128)} %param.11) | copy-start | bytes 196612
  0.9 4.9 %collective-permute-start.1 = (bf16[64,256]{1,0:T(8,128)(2,1)S(1)}, bf16[64,256]{1,0:T(8,128)(2,1)S(1)}, u32[]{:S(2)}, u32[]{:S(2)}) collective-permute-start(bf16[64,256]{1,0:T(8,128)(2,1)S(1)} %shard_map.110), channel_id=1, source_target_pairs={{0,1},{1,0},{2,3},{3,2},{4,5},{5,4},{6,7},{7,6},{8,9},{9,8},{10,11... | collective-permute-start | bytes 98312 | tf_op jit(solution)/shard_map/ppermute | solution.py:322
  5.8 2.9 %copy-start.1 = (f32[4,2,8,256]{3,2,1,0:T(8,128)S(1)}, f32[4,2,8,256]{3,2,1,0:T(8,128)}, u32[]{:S(2)}) copy-start(f32[4,2,8,256]{3,2,1,0:T(8,128)} %param.12) | copy-start | bytes 196612
  5.8 7.8 %collective-permute-start.2 = (bf16[128,256]{1,0:T(8,128)(2,1)S(1)}, bf16[128,256]{1,0:T(8,128)(2,1)S(1)}, u32[]{:S(2)}, u32[]{:S(2)}) collective-permute-start(bf16[128,256]{1,0:T(8,128)(2,1)S(1)} %pad_maximum_fusion.own_ref), channel_id=1, source_target_pairs={{0,2},{2,0},{4,6},{6,4},{8,10},{10,8},{12,14},{14,12},{16,18},{18,... | collective-permute-start | bytes 196616 | tf_op jit(solution)/shard_map/ppermute | solution.py:331
  5.9 7.9 %collective-permute-start.3 = (bf16[128,256]{1,0:T(8,128)(2,1)S(1)}, bf16[128,256]{1,0:T(8,128)(2,1)S(1)}, u32[]{:S(2)}, u32[]{:S(2)}) collective-permute-start(bf16[128,256]{1,0:T(8,128)(2,1)S(1)} %pad_maximum_fusion.own_ref), channel_id=1, source_target_pairs={{2,4},{4,2},{6,8},{8,6},{10,12},{12,10},{14,16},{16,14},{18,20},{2... | collective-permute-start | bytes 196616 | tf_op jit(solution)/shard_map/ppermute | solution.py:330
  8.6 0.7 %copy-start.5 = (s32[1,1,256]{2,1,0:T(1,128)S(1)}, s32[1,1,256]{2,1,0:T(1,128)}, u32[]{:S(2)}) copy-start(s32[1,1,256]{2,1,0:T(1,128)} %param.19) | copy-start | bytes 3076
  8.6 0.7 %copy-start.6 = (s32[1,1,256]{2,1,0:T(1,128)S(1)}, s32[1,1,256]{2,1,0:T(1,128)}, u32[]{:S(2)}) copy-start(s32[1,1,256]{2,1,0:T(1,128)} %param.20) | copy-start | bytes 3076
  8.6 0.7 %copy-start.7 = (f32[1,1,256]{2,1,0:T(1,128)S(1)}, f32[1,1,256]{2,1,0:T(1,128)}, u32[]{:S(2)}) copy-start(f32[1,1,256]{2,1,0:T(1,128)} %param.21) | copy-start | bytes 3076
  8.7 0.7 %copy-start.4 = (s32[1,1,256]{2,1,0:T(1,128)S(1)}, s32[1,1,256]{2,1,0:T(1,128)}, u32[]{:S(2)}) copy-start(s32[1,1,256]{2,1,0:T(1,128)} %param.18) | copy-start | bytes 3076
  9.4 0.8 %copy-start.2 = (bf16[9,96,18]{1,2,0:T(8,128)(2,1)S(1)}, bf16[9,96,18]{1,2,0:T(8,128)(2,1)}, u32[]{:S(2)}) copy-start(bf16[9,96,18]{1,2,0:T(8,128)(2,1)} %param.14) | copy-start | bytes 93316
  9.4 0.7 %copy-start.3 = (bf16[9,2,96]{2,1,0:T(2,128)(2,1)S(1)}, bf16[9,2,96]{2,1,0:T(2,128)(2,1)}, u32[]{:S(2)}) copy-start(bf16[9,2,96]{2,1,0:T(2,128)(2,1)} %conv_out_ref.1) | copy-start | bytes 10372
  9.4 3.9 %collective-permute-start = (bf16[48,256]{1,0:T(8,128)(2,1)S(1)}, bf16[48,256]{1,0:T(8,128)(2,1)S(1)}, u32[]{:S(2)}, u32[]{:S(2)}) collective-permute-start(bf16[48,256]{1,0:T(8,128)(2,1)S(1)} %get-tuple-element.16.msg_ref), channel_id=1, source_target_pairs={{0,1},{1,0},{2,3},{3,2},{4,5},{5,4},{6,7},{7,6},{8,9},{9,8},{10,11... | collective-permute-start | bytes 73736 | tf_op jit(solution)/shard_map/ppermute | solution.py:322
  9.5 0.7 %copy-start.8 = (f32[96]{0:T(128)S(1)}, f32[96]{0:T(128)}, u32[]{:S(2)}) copy-start(f32[96]{0:T(128)} %param.16) | copy-start | bytes 1156
  15.3 4.2 %copy-start.9 = (f32[4,2,8,256]{3,2,1,0:T(8,128)S(1)}, f32[4,2,8,256]{3,2,1,0:T(8,128)}, u32[]{:S(2)}) copy-start(f32[4,2,8,256]{3,2,1,0:T(8,128)} %param.13) | copy-start | bytes 196612
  15.3 1.3 %collective-permute-start.4 = (bf16[96,256]{1,0:T(8,128)(2,1)S(1)}, bf16[96,256]{1,0:T(8,128)(2,1)S(1)}, u32[]{:S(2)}, u32[]{:S(2)}) collective-permute-start(bf16[96,256]{1,0:T(8,128)(2,1)S(1)} %get-tuple-element.22.own_ref), channel_id=1, source_target_pairs={{0,2},{2,0},{4,6},{6,4},{8,10},{10,8},{12,14},{14,12},{16,18},{18,... | collective-permute-start | bytes 147464 | tf_op jit(solution)/shard_map/ppermute | solution.py:331
  15.4 4.2 %collective-permute-start.5 = (bf16[96,256]{1,0:T(8,128)(2,1)S(1)}, bf16[96,256]{1,0:T(8,128)(2,1)S(1)}, u32[]{:S(2)}, u32[]{:S(2)}) collective-permute-start(bf16[96,256]{1,0:T(8,128)(2,1)S(1)} %get-tuple-element.22.own_ref), channel_id=1, source_target_pairs={{2,4},{4,2},{6,8},{8,6},{10,12},{12,10},{14,16},{16,14},{18,20},{2... | collective-permute-start | bytes 147464 | tf_op jit(solution)/shard_map/ppermute | solution.py:330

commit v2 on v1

--- a/solution.py
+++ b/solution.py
@@ -54,7 +54,6 @@
     split_halves(scaled_in, scaled_ref)
     for row in range(0, ROWS, 2):
         pair = jnp.concatenate([row_of(scaled_ref, row), row_of(scaled_ref, row + 1)], axis=0)
-        pair = pair * (1.0 / (1.0 + LEVELS[0] ** 2) ** 0.5)
         msg_ref[row * FL : (row + 2) * FL, :] = pair.astype(BF16)
 
 
@@ -208,8 +207,11 @@
             hid_ref[step * n : (step + 1) * n, :] = (half + half * jnp.tanh(half)).astype(BF16)
         row = step - LAG2
         if 0 <= row < hidden_rows:
-            prod_ref[row * 72 : (row + 1) * 72, :] = jnp.dot(
-                w2_ref[...], hid_ref[row * n : (row + 1) * n, :], preferred_element_type=F32
+            first_off = max(0, row - (hidden_rows - 3))
+            last_off = min(2, row)
+            used = slice(first_off * 24, (last_off + 1) * 24)
+            prod_ref[row * 72 + used.start : row * 72 + used.stop, :] = jnp.dot(
+                w2_ref[used, :], hid_ref[row * n : (row + 1) * n, :], preferred_element_type=F32
             )
         row = step - LAG2 - LAG3
         if row >= 2:
@@ -387,8 +389,9 @@
     line = lambda a: a.reshape(1, -1)
     x, noise_a, noise_b = flat(noisy_states), flat(noise_first), flat(noise_second)
     shape = jax.ShapeDtypeStruct
+    scaled = (x / (1.0 + LEVELS[0] ** 2) ** 0.5).astype(BF16)
     halves = pltpu.VMEM((2 * ROWS * FL, 128), F32)
-    (msg,) = call(pack_kernel, (x,), [VMEM], [shape((ROWS * FL, COLS), BF16)], [halves])
+    (msg,) = call(pack_kernel, (scaled,), [VMEM], [shape((ROWS * FL, COLS), BF16)], [halves])
     grid = shape((ROWS * FL, COLS), F32)
     aux, x_rows, noise_rows = call(
         aux_kernel,

time: 21.6 us -> 21.6 us (level)
  local copies, waits for them, and re-layouts: 2.2 us -> 1.35 us
  other arithmetic: 0.01 us -> 0.85 us
    convert_element_type x0 -> x1, other arithmetic: none -> 0.85 us  [per_device(): scaled = (x / (1.0 + LEVELS[0] ** 2) ** 0.5).astype(BF16)]
    unnamed x20, local copies, waits for them, and re-layouts: 2.19 us -> 1.35 us
where the time goes in v2:
time: 21.6 us; the launch traced here: 21.4 us
  waiting for transfers between devices  8.26 us (38%)
  starting transfers between devices  5.79 us (27%)
  Pallas kernels  4.36 us (20%)
  local copies, waits for them, and re-layouts  1.35 us (6%)
  other arithmetic  0.85 us (4%)
  between operations  0.8 us (4%)
    ppermute x2, waiting for transfers between devices, exchange_rows(): lax.ppermute(block, 'rows', [(i, (i + 1) % n_rows) for i in range(n_rows)])  4.7 us
    pallas_call x8, Pallas kernels, call(): pl.pallas_call(kernel, out_shape=tuple(outs), in_specs=specs, out_specs=t...  4.36 us
    ppermute x2, starting transfers between devices, exchange_rows(): lax.ppermute(block, 'rows', [(i, (i + 1) % n_rows) for i in range(n_rows)])  3.09 us
    ppermute x2, waiting for transfers between devices, exchange_time(): far = lax.ppermute(block, ('tm', 'rows'), far_pairs)  2.81 us
    ppermute x2, starting transfers between devices, exchange_time(): far = lax.ppermute(block, ('tm', 'rows'), far_pairs)  2.55 us
    unnamed x20, local copies, waits for them, and re-layouts  1.35 us
    convert_element_type x1, other arithmetic, per_device(): scaled = (x / (1.0 + LEVELS[0] ** 2) ** 0.5).astype(BF16)  0.85 us
    ppermute x2, waiting for transfers between devices, exchange_time(): core = lax.ppermute(block, ('tm', 'rows'), core_pairs)  0.75 us
  transfers between devices with their start and end apart: 6, of which 4 were waited for; matrix products, arithmetic and copies ran while one was open for 0% of the time, Pallas kernels for 4%

profile of v2, /device:TPU:0, one launch (start us, length us, event | category | flops | bytes accessed | tf_op | source)
XLA Modules:
  0.0 21.4 jit_solution(2384212930355088181)
XLA Ops:
  0.0 0.8 %multiply_convert_fusion.scaled_in = bf16[64,256]{1,0:T(8,128)(2,1)S(1)} fusion(f32[4,2,8,256]{3,2,1,0:T(8,128)} %param.11), kind=kLoop, calls=%fused_computation.1 | loop fusion | flops 32768 | bytes 98304 | tf_op jit(solution)/shard_map/convert_element_type | solution.py:392
  0.9 3.0 %collective-permute-start.1 = (bf16[64,256]{1,0:T(8,128)(2,1)S(1)}, bf16[64,256]{1,0:T(8,128)(2,1)S(1)}, u32[]{:S(2)}, u32[]{:S(2)}) collective-permute-start(bf16[64,256]{1,0:T(8,128)(2,1)S(1)} %shard_map.110), channel_id=1, source_target_pairs={{0,1},{1,0},{2,3},{3,2},{4,5},{5,4},{6,7},{7,6},{8,9},{9,8},{10,11... | collective-permute-start | bytes 98312 | tf_op jit(solution)/shard_map/ppermute | solution.py:324
  3.9 1.9 %collective-permute-done.1 = bf16[64,256]{1,0:T(8,128)(2,1)S(1)} collective-permute-done((bf16[64,256]{1,0:T(8,128)(2,1)S(1)}, bf16[64,256]{1,0:T(8,128)(2,1)S(1)}, u32[]{:S(2)}, u32[]{:S(2)}) %collective-permute-start.1) | collective-permute-done | bytes 32800 | tf_op jit(solution)/shard_map/ppermute | solution.py:324
  5.8 0.0 copy-start
  5.8 0.0 copy-start.1
  5.8 0.1 collective-permute-start.2
  5.9 2.1 %collective-permute-start.3 = (bf16[128,256]{1,0:T(8,128)(2,1)S(1)}, bf16[128,256]{1,0:T(8,128)(2,1)S(1)}, u32[]{:S(2)}, u32[]{:S(2)}) collective-permute-start(bf16[128,256]{1,0:T(8,128)(2,1)S(1)} %pad_maximum_fusion.own_ref), channel_id=1, source_target_pairs={{2,4},{4,2},{6,8},{8,6},{10,12},{12,10},{14,16},{16,14},{18,20},{2... | collective-permute-start | bytes 196616 | tf_op jit(solution)/shard_map/ppermute | solution.py:332
  8.6 0.0 copy-start.5
  8.7 0.0 copy-start.6
  8.7 0.0 copy-start.7
  8.7 0.0 copy-start.4
  8.7 0.0 copy-done
  8.7 0.0 copy-done.1
  8.7 0.6 %copy-done.5 = s32[1,1,256]{2,1,0:T(1,128)S(1)} copy-done((s32[1,1,256]{2,1,0:T(1,128)S(1)}, s32[1,1,256]{2,1,0:T(1,128)}, u32[]{:S(2)}) %copy-start.5) | copy-done | bytes 1048
  9.3 0.0 copy-done.6
  9.3 0.0 copy-done.7
  9.4 0.0 copy-done.4
  9.4 0.0 copy-start.2
  9.4 0.1 shard_map.109
  9.5 0.0 copy-start.3
  9.5 0.1 collective-permute-start
  9.5 0.0 copy-start.8
  9.5 0.6 %copy-done.2 = bf16[9,96,18]{1,2,0:T(8,128)(2,1)S(1)} copy-done((bf16[9,96,18]{1,2,0:T(8,128)(2,1)S(1)}, bf16[9,96,18]{1,2,0:T(8,128)(2,1)}, u32[]{:S(2)}) %copy-start.2) | copy-done | bytes 31128
  10.2 0.0 copy-done.3
  10.2 0.0 copy-done.8
  10.2 0.3 %shard_map.112 = (bf16[384,240]{1,0:T(8,128)(2,1)S(1)}, bf16[72,384]{1,0:T(8,128)(2,1)S(1)}) custom-call(bf16[9,18,96]{2,1,0:T(8,128)(2,1)S(1)} %bitcast.13, bf16[9,2,96]{2,1,0:T(2,128)(2,1)S(1)} %copy-done.3, f32[1,96]{1,0:T(1,128)S(1)} %bitcast.18), custom_call_target="tpu_custom_call" | custom-call | bytes 274560 | tf_op jit(solution)/shard_map/pallas_call | solution.py:299
  10.5 2.8 %collective-permute-done.up_ref.down_ref.aux_up_ref.aux_down_ref = bf16[48,256]{1,0:T(8,128)(2,1)S(1)} collective-permute-done((bf16[48,256]{1,0:T(8,128)(2,1)S(1)}, bf16[48,256]{1,0:T(8,128)(2,1)S(1)}, u32[]{:S(2)}, u32[]{:S(2)}) %collective-permute-start) | collective-permute-done | bytes 24608 | tf_op jit(solution)/shard_map/ppermute | solution.py:324
  13.3 0.3 %shard_map.113 = (f32[96,256]{1,0:T(8,128)S(1)}, f32[96,256]{1,0:T(8,128)S(1)}) custom-call(bf16[48,256]{1,0:T(8,128)(2,1)S(1)} %get-tuple-element.16.msg_ref, bf16[48,256]{1,0:T(8,128)(2,1)S(1)} %collective-permute-done.up_ref.down_ref.aux_up_ref.aux_down_ref, bf16[48,256]{1,0:T(8,128)(2,1)S(1)} %collective-permute-done.up_ref.down_ref.aux_up_ref.aux_down_ref), custom_call_target="tpu_custom_call" | custom-call | bytes 270336 | tf_op jit(solution)/shard_map/pallas_call | solution.py:299
  13.6 0.0 collective-permute-done.2.core_ref
  13.6 0.1 shard_map.111.near_ref
  13.8 0.0 collective-permute-done.3.far_ref
  13.8 1.6 %shard_map.114 = (f32[64,256]{1,0:T(8,128)S(1)}, bf16[96,256]{1,0:T(8,128)(2,1)S(1)}) custom-call(f32[64,256]{1,0:T(8,128)S(1)} %get-tuple-element.14.x_ref, f32[64,256]{1,0:T(8,128)S(1)} %get-tuple-element.15.noise_ref, bf16[48,256]{1,0:T(8,128)(2,1)S(1)} %collective-permute-done.up_ref.down_ref.aux_up_ref.aux_down_ref, ...), custom_call_target="tpu_custom_call" | custom-call | flops 902823936 | bytes 1255424 | tf_op jit(solution)/shard_map/pallas_call | solution.py:299
  15.3 0.0 copy-start.9
  15.3 0.1 collective-permute-start.4
  15.4 0.5 %collective-permute-start.5 = (bf16[96,256]{1,0:T(8,128)(2,1)S(1)}, bf16[96,256]{1,0:T(8,128)(2,1)S(1)}, u32[]{:S(2)}, u32[]{:S(2)}) collective-permute-start(bf16[96,256]{1,0:T(8,128)(2,1)S(1)} %get-tuple-element.22.own_ref), channel_id=1, source_target_pairs={{2,4},{4,2},{6,8},{8,6},{10,12},{12,10},{14,16},{16,14},{18,20},{2... | collective-permute-start | bytes 147464 | tf_op jit(solution)/shard_map/ppermute | solution.py:332
  15.9 0.7 %collective-permute-done.4.core_ref = bf16[96,256]{1,0:T(8,128)(2,1)S(1)} collective-permute-done((bf16[96,256]{1,0:T(8,128)(2,1)S(1)}, bf16[96,256]{1,0:T(8,128)(2,1)S(1)}, u32[]{:S(2)}, u32[]{:S(2)}) %collective-permute-start.4) | collective-permute-done | bytes 49184 | tf_op jit(solution)/shard_map/ppermute | solution.py:333
  16.6 0.1 shard_map.115.near_ref
  16.8 2.8 %collective-permute-done.5.far_ref = bf16[96,256]{1,0:T(8,128)(2,1)S(1)} collective-permute-done((bf16[96,256]{1,0:T(8,128)(2,1)S(1)}, bf16[96,256]{1,0:T(8,128)(2,1)S(1)}, u32[]{:S(2)}, u32[]{:S(2)}) %collective-permute-start.5) | collective-permute-done | bytes 49184 | tf_op jit(solution)/shard_map/ppermute | solution.py:332
  19.6 0.0 copy-done.9
  19.6 1.8 %shard_map.116 = f32[64,256]{1,0:T(8,128)} custom-call(f32[64,256]{1,0:T(8,128)S(1)} %get-tuple-element.21.x_ref, f32[64,256]{1,0:T(8,128)S(1)} %bitcast.19, bf16[576,256]{1,0:T(8,128)(2,1)S(1)} %shard_map.115.near_ref, bf16[96,256]{1,0:T(8,128)(2,1)S(1)} %collective-permute-done.5.far_ref, bf16[384,240]{1,0:T(8,128)(2,1)S(1)} %get-tuple-element.17.w1_ref, ...), custom_call_target="tpu_custom_call" | custom-call | flops 644874240 | bytes 976896 | tf_op jit(solution)/shard_map/pallas_call | solution.py:299
  (3 shorter events, 0.0 us)
Async XLA Ops:
  0.9 4.9 %collective-permute-start.1 = (bf16[64,256]{1,0:T(8,128)(2,1)S(1)}, bf16[64,256]{1,0:T(8,128)(2,1)S(1)}, u32[]{:S(2)}, u32[]{:S(2)}) collective-permute-start(bf16[64,256]{1,0:T(8,128)(2,1)S(1)} %shard_map.110), channel_id=1, source_target_pairs={{0,1},{1,0},{2,3},{3,2},{4,5},{5,4},{6,7},{7,6},{8,9},{9,8},{10,11... | collective-permute-start | bytes 98312 | tf_op jit(solution)/shard_map/ppermute | solution.py:324
  5.8 2.9 %copy-start = (f32[4,2,8,256]{3,2,1,0:T(8,128)S(1)}, f32[4,2,8,256]{3,2,1,0:T(8,128)}, u32[]{:S(2)}) copy-start(f32[4,2,8,256]{3,2,1,0:T(8,128)} %param.11) | copy-start | bytes 196612
  5.8 2.9 %copy-start.1 = (f32[4,2,8,256]{3,2,1,0:T(8,128)S(1)}, f32[4,2,8,256]{3,2,1,0:T(8,128)}, u32[]{:S(2)}) copy-start(f32[4,2,8,256]{3,2,1,0:T(8,128)} %param.12) | copy-start | bytes 196612
  5.8 7.8 %collective-permute-start.2 = (bf16[128,256]{1,0:T(8,128)(2,1)S(1)}, bf16[128,256]{1,0:T(8,128)(2,1)S(1)}, u32[]{:S(2)}, u32[]{:S(2)}) collective-permute-start(bf16[128,256]{1,0:T(8,128)(2,1)S(1)} %pad_maximum_fusion.own_ref), channel_id=1, source_target_pairs={{0,2},{2,0},{4,6},{6,4},{8,10},{10,8},{12,14},{14,12},{16,18},{18,... | collective-permute-start | bytes 196616 | tf_op jit(solution)/shard_map/ppermute | solution.py:333
  5.9 7.9 %collective-permute-start.3 = (bf16[128,256]{1,0:T(8,128)(2,1)S(1)}, bf16[128,256]{1,0:T(8,128)(2,1)S(1)}, u32[]{:S(2)}, u32[]{:S(2)}) collective-permute-start(bf16[128,256]{1,0:T(8,128)(2,1)S(1)} %pad_maximum_fusion.own_ref), channel_id=1, source_target_pairs={{2,4},{4,2},{6,8},{8,6},{10,12},{12,10},{14,16},{16,14},{18,20},{2... | collective-permute-start | bytes 196616 | tf_op jit(solution)/shard_map/ppermute | solution.py:332
  8.6 0.7 %copy-start.5 = (s32[1,1,256]{2,1,0:T(1,128)S(1)}, s32[1,1,256]{2,1,0:T(1,128)}, u32[]{:S(2)}) copy-start(s32[1,1,256]{2,1,0:T(1,128)} %param.19) | copy-start | bytes 3076
  8.7 0.7 %copy-start.6 = (s32[1,1,256]{2,1,0:T(1,128)S(1)}, s32[1,1,256]{2,1,0:T(1,128)}, u32[]{:S(2)}) copy-start(s32[1,1,256]{2,1,0:T(1,128)} %param.20) | copy-start | bytes 3076
  8.7 0.7 %copy-start.7 = (f32[1,1,256]{2,1,0:T(1,128)S(1)}, f32[1,1,256]{2,1,0:T(1,128)}, u32[]{:S(2)}) copy-start(f32[1,1,256]{2,1,0:T(1,128)} %param.21) | copy-start | bytes 3076
  8.7 0.7 %copy-start.4 = (s32[1,1,256]{2,1,0:T(1,128)S(1)}, s32[1,1,256]{2,1,0:T(1,128)}, u32[]{:S(2)}) copy-start(s32[1,1,256]{2,1,0:T(1,128)} %param.18) | copy-start | bytes 3076
  9.4 0.8 %copy-start.2 = (bf16[9,96,18]{1,2,0:T(8,128)(2,1)S(1)}, bf16[9,96,18]{1,2,0:T(8,128)(2,1)}, u32[]{:S(2)}) copy-start(bf16[9,96,18]{1,2,0:T(8,128)(2,1)} %param.14) | copy-start | bytes 93316
  9.5 0.7 %copy-start.3 = (bf16[9,2,96]{2,1,0:T(2,128)(2,1)S(1)}, bf16[9,2,96]{2,1,0:T(2,128)(2,1)}, u32[]{:S(2)}) copy-start(bf16[9,2,96]{2,1,0:T(2,128)(2,1)} %conv_out_ref.1) | copy-start | bytes 10372
  9.5 3.9 %collective-permute-start = (bf16[48,256]{1,0:T(8,128)(2,1)S(1)}, bf16[48,256]{1,0:T(8,128)(2,1)S(1)}, u32[]{:S(2)}, u32[]{:S(2)}) collective-permute-start(bf16[48,256]{1,0:T(8,128)(2,1)S(1)} %get-tuple-element.16.msg_ref), channel_id=1, source_target_pairs={{0,1},{1,0},{2,3},{3,2},{4,5},{5,4},{6,7},{7,6},{8,9},{9,8},{10,11... | collective-permute-start | bytes 73736 | tf_op jit(solution)/shard_map/ppermute | solution.py:324
  9.5 0.7 %copy-start.8 = (f32[96]{0:T(128)S(1)}, f32[96]{0:T(128)}, u32[]{:S(2)}) copy-start(f32[96]{0:T(128)} %param.16) | copy-start | bytes 1156
  15.3 4.2 %copy-start.9 = (f32[4,2,8,256]{3,2,1,0:T(8,128)S(1)}, f32[4,2,8,256]{3,2,1,0:T(8,128)}, u32[]{:S(2)}) copy-start(f32[4,2,8,256]{3,2,1,0:T(8,128)} %param.13) | copy-start | bytes 196612
  15.3 1.3 %collective-permute-start.4 = (bf16[96,256]{1,0:T(8,128)(2,1)S(1)}, bf16[96,256]{1,0:T(8,128)(2,1)S(1)}, u32[]{:S(2)}, u32[]{:S(2)}) collective-permute-start(bf16[96,256]{1,0:T(8,128)(2,1)S(1)} %get-tuple-element.22.own_ref), channel_id=1, source_target_pairs={{0,2},{2,0},{4,6},{6,4},{8,10},{10,8},{12,14},{14,12},{16,18},{18,... | collective-permute-start | bytes 147464 | tf_op jit(solution)/shard_map/ppermute | solution.py:333
  15.4 4.2 %collective-permute-start.5 = (bf16[96,256]{1,0:T(8,128)(2,1)S(1)}, bf16[96,256]{1,0:T(8,128)(2,1)S(1)}, u32[]{:S(2)}, u32[]{:S(2)}) collective-permute-start(bf16[96,256]{1,0:T(8,128)(2,1)S(1)} %get-tuple-element.22.own_ref), channel_id=1, source_target_pairs={{2,4},{4,2},{6,8},{8,6},{10,12},{12,10},{14,16},{16,14},{18,20},{2... | collective-permute-start | bytes 147464 | tf_op jit(solution)/shard_map/ppermute | solution.py:332
